TPU v7x, 128 devices: a whole 4x4x4 slice. The times are simulated.
128 devices in a mesh: req: 4 (over x), exp: 32 (over y, z, core).
Axes of the slice: x: 4, y: 4, z: 4, core: 2. Of those that a mesh axis runs over, the one named last changes fastest.
Arguments:
- tokens: bfloat16 [32768, 1536], P(('req', 'exp')), may hold values from -6 to 6
- token_request_slot: int32 [128, 256], P(('req', 'exp')), may hold values from 0 to 3, never falling along the last dimension, each value on 1 to 128 neighbouring positions
- request_prompt: int32 [512], P(('req', 'exp')), may hold values from 0 to 31
- request_adapter: int32 [512], P(('req', 'exp')), may hold values from 0 to 15
- prompt_page_table: int32 [512], replicated, may hold values from 0 to 511, each once
- shared_prompt_cache: bfloat16 [512, 16, 512], P(('req', 'exp')), may hold values from -180 to 180
- routes: int32 [32768, 4], P(('req', 'exp')), may hold values from 0 to 31, all different within a row; in each aligned block of 256 rows (0 to 255, 256 to 511, ...) at most 48 rows name the same one
- attention_norm_gain: bfloat16 [1536], replicated, may hold values from 0.099609375 to 1.8984375
- query_matrix: bfloat16 [1536, 1536], replicated, may hold values from -0.15625 to 0.15625
- key_value_weight: bfloat16 [1536, 512], replicated, may hold values from -0.15625 to 0.15625
- attention_output_weight: bfloat16 [1536, 1536], replicated, may hold values from -0.15625 to 0.15625
- adapter_query_down: bfloat16 [1536, 256], replicated, may hold values from -0.15625 to 0.15625
- adapter_query_up: bfloat16 [256, 1536], replicated, may hold values from -1.5 to 1.5
- adapter_output_down: bfloat16 [1536, 256], replicated, may hold values from -0.15625 to 0.15625
- adapter_output_up: bfloat16 [256, 1536], replicated, may hold values from -1.5 to 1.5
- expert_norm_gain: bfloat16 [1536], replicated, may hold values from 0.099609375 to 1.8984375
- router: bfloat16 [1536, 32], replicated, may hold values from -0.15625 to 0.15625
- expert_gate_up: bfloat16 [32, 1536, 1536], P('exp'), may hold values from -0.15625 to 0.15625
- expert_down: bfloat16 [32, 768, 1536], P('exp'), may hold values from -0.21875 to 0.21875
Outputs:
- mixed_rows: bfloat16 [32768, 1536], P(('req', 'exp'))
Inputs may be any that keep to these rules, and one draw needn't show every extreme that they name: `token_request_slot`: along a device's row the slots never fall; each of the 4 slots holds 1 to 128 tokens and one holds exactly 128. `prompt_page_table`: the entries whose index divided by 16 (rounded down) is p are the pages of prompt p in order; every page appears once. `routes`: each token names 4 different experts. Among the tokens of one device no expert is named more than 48 times, and in every draw some device's tokens name some expert exactly 48 times.
All inputs are finite; a program needn't handle non-finite values.
Results may differ from a plain program's by a relative error of at most 0.017.
The roundings to bfloat16 on the way count: a program that leaves them out, or rounds other values in their place, can miss the bound.
Values may be sent and summed in bfloat16 or wider, within the bound.
A program may use at most 128 MiB of HBM per device.

v0:
```python
import jax
import jax.numpy as jnp
from jax import lax
from jax.sharding import PartitionSpec as P

QUERY_HEADS = 12
KEY_VALUE_HEADS = 2
HEAD_WIDTH = 128
TOPK = 4
ADAPTER_RANK = 16
PPP = 16
PROMPT_LENGTH = 256
EPSILON = 1e-06
THETA = 1000000.0
VERY_NEGATIVE = -1e30


def rms_norm(weight_matrix, gain_vector):
    values = weight_matrix.astype(jnp.float32)
    factor = lax.rsqrt(jnp.mean(values * values, axis=-1, keepdims=True) + EPSILON)
    return (values * factor * gain_vector.astype(jnp.float32)).astype(jnp.bfloat16)


def apply_rotary(values, token_positions):
    half_width = values.shape[-1] // 2
    frequency = THETA ** (-jnp.arange(half_width).astype(jnp.float32) / half_width)
    angles = token_positions.astype(jnp.float32)[:, None] * frequency[None, :]
    cosine = jnp.cos(angles)[:, None, :]
    sine_table = jnp.sin(angles)[:, None, :]
    first_half = values[..., :half_width]
    second = values[..., half_width:]
    return jnp.concatenate(
        [first_half * cosine - second * sine_table, second * cosine + first_half * sine_table],
        axis=-1,
    )


def adapter_update(weight_matrix, down_proj, up_proj, token_adapter):
    inner = jnp.dot(weight_matrix, down_proj, preferred_element_type=jnp.float32)
    owner_slot = jnp.arange(down_proj.shape[1], dtype=jnp.int32) // ADAPTER_RANK
    inner = jnp.where(owner_slot[None, :] == token_adapter[:, None], inner, 0.0).astype(
        jnp.bfloat16
    )
    return jnp.dot(inner, up_proj, preferred_element_type=jnp.float32)


def request_info(request_row, prompt_req, adapter_req):
    new_token_count = request_row.shape[0]
    request_slot_count = prompt_req.shape[0]
    matches = request_row[:, None] == jnp.arange(request_slot_count, dtype=jnp.int32)[None, :]
    token_adapter = jnp.sum(jnp.where(matches, adapter_req[None, :], 0), axis=1)
    prompt_tok = jnp.sum(jnp.where(matches, prompt_req[None, :], 0), axis=1)
    token_index = jnp.arange(new_token_count, dtype=jnp.int32)
    first_row = jnp.min(jnp.where(matches, token_index[:, None], new_token_count), axis=0)
    start_tok = jnp.sum(jnp.where(matches, first_row[None, :], 0), axis=1)
    token_positions = PROMPT_LENGTH + token_index - start_tok
    return (token_adapter, prompt_tok, token_positions)


def apply_projection(
    tokens,
    token_adapter,
    token_positions,
    attention_norm_gain,
    query_matrix,
    key_value_weight,
    adapter_query_down,
    adapter_query_up,
):
    new_token_count = tokens.shape[0]
    normalized = rms_norm(tokens, attention_norm_gain)
    query_rows = jnp.dot(normalized, query_matrix, preferred_element_type=jnp.float32)
    query_rows = query_rows + adapter_update(
        normalized, adapter_query_down, adapter_query_up, token_adapter
    )
    query_rows = apply_rotary(
        query_rows.reshape(new_token_count, QUERY_HEADS, HEAD_WIDTH), token_positions
    ).astype(jnp.bfloat16)
    key_value_rows = jnp.dot(
        normalized, key_value_weight, preferred_element_type=jnp.float32
    ).reshape(new_token_count, 2 * KEY_VALUE_HEADS, HEAD_WIDTH)
    key_matrix = apply_rotary(key_value_rows[:, :KEY_VALUE_HEADS], token_positions).astype(
        jnp.bfloat16
    )
    value_matrix = key_value_rows[:, KEY_VALUE_HEADS:].astype(jnp.bfloat16)
    return (query_rows, key_matrix, value_matrix)


def finalize(
    attention_output,
    tokens,
    token_adapter,
    attention_output_weight,
    adapter_output_down,
    adapter_output_up,
):
    expert_mixture = jnp.dot(
        attention_output, attention_output_weight, preferred_element_type=jnp.float32
    )
    expert_mixture = expert_mixture + adapter_update(
        attention_output, adapter_output_down, adapter_output_up, token_adapter
    )
    return (tokens.astype(jnp.float32) + expert_mixture).astype(jnp.bfloat16)


def gate_weights(ffn_normed, router, routes):
    logits = jnp.dot(ffn_normed, router, preferred_element_type=jnp.float32)
    picked = jnp.take_along_axis(logits, routes, axis=1)
    squashed = jax.nn.sigmoid(picked)
    return squashed / jnp.sum(squashed, axis=1, keepdims=True)


def slot_of(routes, experts, capacity):
    flat_routes = routes.reshape(-1)
    onehot = (flat_routes[:, None] == jnp.arange(experts, dtype=jnp.int32)[None, :]).astype(
        jnp.int32
    )
    before = jnp.cumsum(onehot, axis=0) - onehot
    rank_pick = jnp.sum(before * onehot, axis=1)
    return flat_routes * capacity + rank_pick


def block_attention(running, grouped_queries, key_matrix, value_matrix, allowed):
    running_max, totals, accum = running
    scale = grouped_queries.shape[-1] ** (-0.5)
    scores = (
        jnp.einsum(
            "tkgd,nkd->tkgn", grouped_queries, key_matrix, preferred_element_type=jnp.float32
        )
        * scale
    )
    scores = jnp.where(allowed[:, None, None, :], scores, VERY_NEGATIVE)
    new_max = jnp.maximum(running_max, jnp.max(scores, axis=-1))
    factor = jnp.exp(running_max - new_max)
    weights = jnp.exp(scores - new_max[..., None])
    totals = totals * factor + jnp.sum(weights, axis=-1)
    summed = jnp.einsum(
        "tkgn,nkd->tkgd",
        weights.astype(jnp.bfloat16),
        value_matrix,
        preferred_element_type=jnp.float32,
    )
    accum = accum * factor[..., None] + summed
    return (new_max, totals, accum)


def on_device(
    tokens,
    token_request_slot,
    request_prompt,
    request_adapter,
    prompt_page_table,
    shared_prompt_cache,
    routes,
    attention_norm_gain,
    query_matrix,
    key_value_weight,
    attention_output_weight,
    adapter_query_down,
    adapter_query_up,
    adapter_output_down,
    adapter_output_up,
    expert_norm_gain,
    router,
    expert_gate_up,
    expert_down,
):
    new_token_count = tokens.shape[0]
    request_row = token_request_slot[0]
    request_slot_count = request_prompt.shape[0]
    token_adapter, prompt_tok, token_positions = request_info(
        request_row, request_prompt, request_adapter
    )
    query_rows, key_matrix, value_matrix = apply_projection(
        tokens,
        token_adapter,
        token_positions,
        attention_norm_gain,
        query_matrix,
        key_value_weight,
        adapter_query_down,
        adapter_query_up,
    )
    query_group_width = QUERY_HEADS // KEY_VALUE_HEADS
    grouped_queries = query_rows.reshape(
        new_token_count, KEY_VALUE_HEADS, query_group_width, HEAD_WIDTH
    )
    token_index = jnp.arange(new_token_count, dtype=jnp.int32)
    local_ok = (request_row[:, None] == request_row[None, :]) & (
        token_index[None, :] <= token_index[:, None]
    )
    initial = (
        jnp.full((new_token_count, KEY_VALUE_HEADS, query_group_width), VERY_NEGATIVE, jnp.float32),
        jnp.zeros((new_token_count, KEY_VALUE_HEADS, query_group_width), jnp.float32),
        jnp.zeros((new_token_count, KEY_VALUE_HEADS, query_group_width, HEAD_WIDTH), jnp.float32),
    )
    running_progress = block_attention(initial, grouped_queries, key_matrix, value_matrix, local_ok)
    requested_pages = jnp.take(prompt_page_table.reshape(-1, PPP), request_prompt, axis=0).reshape(
        -1
    )
    complete_cache = lax.all_gather(shared_prompt_cache, ("req", "exp"), axis=0, tiled=True)
    page_token_rows = jnp.take(complete_cache, requested_pages, axis=0).reshape(
        request_slot_count * PROMPT_LENGTH, 2 * KEY_VALUE_HEADS, HEAD_WIDTH
    )
    owner_slot = jnp.arange(request_slot_count * PROMPT_LENGTH, dtype=jnp.int32) // PROMPT_LENGTH
    prompt_valid_mask = request_row[:, None] == owner_slot[None, :]
    running_progress = block_attention(
        running_progress,
        grouped_queries,
        page_token_rows[:, :KEY_VALUE_HEADS],
        page_token_rows[:, KEY_VALUE_HEADS:],
        prompt_valid_mask,
    )
    running_max, totals, accum = running_progress
    attention_output = (
        (accum / totals[..., None])
        .reshape(new_token_count, QUERY_HEADS * HEAD_WIDTH)
        .astype(jnp.bfloat16)
    )
    hidden_state = finalize(
        attention_output,
        tokens,
        token_adapter,
        attention_output_weight,
        adapter_output_down,
        adapter_output_up,
    )
    ffn_normed = rms_norm(hidden_state, expert_norm_gain)
    gates = gate_weights(ffn_normed, router, routes)
    local_experts = expert_gate_up.shape[0]
    experts = local_experts * lax.axis_size("exp")
    capacity = 3 * new_token_count * TOPK // (2 * experts)
    destination = slot_of(routes, experts, capacity)
    slot_total = experts * capacity
    matches = jnp.arange(slot_total, dtype=jnp.int32)[:, None] == destination[None, :]
    source = jnp.arange(new_token_count * TOPK, dtype=jnp.int32) // TOPK
    source_tok = jnp.sum(jnp.where(matches, source[None, :], 0), axis=1)
    filled = jnp.any(matches, axis=1)
    outgoing = jnp.where(
        filled[:, None], jnp.take(ffn_normed, source_tok, axis=0), jnp.zeros((), jnp.bfloat16)
    )
    outgoing = outgoing.reshape(experts, capacity, -1)
    arrived = lax.all_to_all(outgoing, "exp", split_axis=0, concat_axis=0, tiled=True)
    sources = arrived.shape[0] // local_experts
    item_count = arrived.shape[1]
    arranged = arrived.reshape(sources, local_experts, item_count, -1)
    inner = jnp.einsum(
        "sxcd,xdf->sxcf", arranged, expert_gate_up, preferred_element_type=jnp.float32
    )
    half_width = inner.shape[-1] // 2
    units = (jax.nn.relu(inner[..., :half_width]) * inner[..., half_width:]).astype(jnp.bfloat16)
    result = jnp.einsum(
        "sxcf,xfd->sxcd", units, expert_down, preferred_element_type=jnp.float32
    ).astype(jnp.bfloat16)
    result = result.reshape(sources * local_experts, item_count, -1)
    returned = lax.all_to_all(result, "exp", split_axis=0, concat_axis=0, tiled=True)
    picked = jnp.take(returned.reshape(slot_total, -1), destination, axis=0).astype(jnp.float32)
    picked = picked.reshape(new_token_count, TOPK, -1)
    mixed_rows = hidden_state.astype(jnp.float32) + jnp.sum(gates[..., None] * picked, axis=1)
    return mixed_rows.astype(jnp.bfloat16)


def solution(mesh):
    return jax.shard_map(
        on_device,
        mesh=mesh,
        in_specs=(
            P(("req", "exp"), None),
            P(("req", "exp"), None),
            P(("req", "exp")),
            P(("req", "exp")),
            P(),
            P(("req", "exp"), None, None),
            P(("req", "exp"), None),
            P(),
            P(),
            P(),
            P(),
            P(),
            P(),
            P(),
            P(),
            P(),
            P(),
            P("exp", None, None),
            P("exp", None, None),
        ),
        out_specs=P(("req", "exp"), None),
        check_vma=False,
    )
```

profile of v0, /device:TPU:32, one launch (start us, length us, event | category | flops | bytes accessed | tf_op | source)
XLA Modules:
  0.0 310.3 jit_solution(16378191095570078321)
XLA Ops:
  7.3 0.8 reshape.426
  10.7 0.8 copy.111
  12.4 1.3 convert_element_type.97
  14.4 9.0 %reduce-window.6 = s32[32,8,128]{2,1,0:T(8,128)S(1)} reduce-window(s32[32,8,128]{2,1,0:T(8,128)S(1)} %fusion.53, s32[]{:T(128)} %constant.133.clone.1), window={size=1x1x128 pad=0_0x0_0x127_0}, to_apply=%region_10.11 | reduce-window | flops 4161536 | bytes 262148 | tf_op jit(solution)/shard_map/reduce-window
  24.5 0.8 fusion.3
  26.8 0.8 select_reduce_fusion.3
  27.6 0.8 select_reduce_fusion.1
  28.8 0.7 copy.97
  30.2 1.4 fusion.19
  31.6 2.8 fusion.75
  34.5 2.0 reshape.424
  36.5 1.2 slice.62
  37.6 0.8 copy.128
  38.4 4.9 %fusion.73 = f32[256,1536]{1,0:T(8,128)} fusion(bf16[1536,1536]{1,0:T(8,128)(2,1)} %param.27, bf16[256,1536]{1,0:T(8,128)(2,1)S(1)} %copy-done.4, f32[1536]{0:T(1024)S(1)} %convert_element_type.85, f32[256]{0:T(256)S(1)} %add_rsqrt_fusion.1), kind=kOutput, calls=%fused_computation.157 | convolution fusion | flops 1209532416 | bytes 7085056 | tf_op jit(solution)/shard_map/dot_general | solution.py:72
  43.3 4.1 %convolution_add_fusion.1 = f32[256,1536]{1,0:T(8,128)} fusion(f32[256,1536]{1,0:T(8,128)} %fusion.73, bf16[256,1536]{1,0:T(8,128)(2,1)} %param.31, bf16[1536,256]{1,0:T(8,128)(2,1)} %param.30, s32[256]{0:T(256)S(1)} %and_select_fusion, s32[256]{0:T(256)S(1)} %get-tuple-element.5, bf16[256,1536]{1,0:T(8,128)(2,1)S(1)} %copy-done.4, ...), kind=kOutput, calls=%fused_computation.27 | convolution fusion | flops 404815872 | bytes 5514240 | tf_op jit(solution)/shard_map/dot_general | solution.py:44
  47.5 3.2 %copy.100 = f32[256,1536]{0,1:T(8,128)} copy(f32[256,1536]{1,0:T(8,128)} %convolution_add_fusion.1) | data formatting | bytes 3145728 | tf_op jit(solution)/shard_map/add | solution.py:73
  50.7 2.3 subtract_convert_fusion
  53.0 1.4 copy.101
  54.4 1.2 copy.102
  56.9 0.9 fusion.38
  57.7 0.9 broadcast_compare_fusion
  58.6 1.5 fusion.77
  60.2 1.0 subtract_convert_fusion.1
  61.2 3.9 %fusion.14 = (f32[256,2,6]{0,2,1:T(8,128)S(1)}, f32[2,256,256,6]{2,1,3,0:T(8,128)}) fusion(pred[256,256]{0,1:T(8,128)(4,1)S(1)} %fusion.38, bf16[256,2,6,64]{3,0,2,1:T(8,128)(2,1)} %bitcast.121, bf16[256,2,6,64]{3,0,2,1:T(8,128)(2,1)S(1)} %bitcast.119, bf16[256,2,64]{2,0,1:T(8,128)(2,1)S(1)} %get-tuple-element.14, bf16[256,2,64]{2,0,1:T(8,128)(2,1)S(1)} %get-tuple-element.13), kind=kOutput, calls=%fused_computation.32 | convolution fusion | flops 205517824 | bytes 4141056 | tf_op jit(solution)/shard_map/tkgd,nkd->tkgn/dot_general | solution.py:127
  65.1 15.9 %all-gather.2.cloned.1.call-done = bf16[512,16,512]{2,1,0:T(8,128)(2,1)} async-done(((bf16[4,16,512]{2,1,0:T(8,128)(2,1)}), bf16[512,16,512]{2,1,0:T(8,128)(2,1)}) %all-gather.2.cloned.1.call-update) | async-done | bytes 8388624 | tf_op jit(solution)/shard_map/all_gather | solution.py:201
  81.1 5.0 %gather_fusion.1 = bf16[64,16,512]{2,1,0:T(8,128)(2,1)} fusion(bf16[512,16,512]{2,1,0:T(8,128)(2,1)} %all-gather.2.cloned.1.call-done, s32[1024]{0:T(1024)S(1)} %pad_clamp_fusion.1), kind=kCustom, calls=%fused_computation.1 | custom fusion | bytes 2097408 | tf_op jit(solution)/shard_map/jit(_take)/gather | solution.py:202
  86.0 2.2 gather.28
  88.2 1.4 copy_select_fusion
  89.7 3.8 %fusion.2 = (f32[256,2,6]{0,2,1:T(8,128)S(1)}, f32[2,1024,256,6]{2,1,3,0:T(8,128)S(1)}) fusion(pred[256,1024]{0,1:T(8,128)(4,1)S(1)} %broadcast_compare_fusion, bf16[256,2,6,64]{3,0,2,1:T(8,128)(2,1)} %bitcast.122, bf16[256,2,6,64]{3,0,2,1:T(8,128)(2,1)S(1)} %bitcast.120, bf16[1024,4,128]{2,0,1:T(8,128)(2,1)S(1)} %copy_select_fusion), kind=kOutput, calls=%fused_computation.9 | convolution fusion | flops 816313344 | bytes 14561280 | tf_op jit(solution)/shard_map/tkgd,nkd->tkgn/dot_general | solution.py:127
  94.4 2.1 fusion.22
  96.4 2.5 fusion
  99.0 4.4 %fusion.25 = bf16[256,2,6,128]{0,3,2,1:T(8,128)(2,1)S(1)} fusion(f32[2,128,256,6]{2,1,3,0:T(8,128)} %fusion.22, f32[2,1024,256,6]{2,1,3,0:T(8,128)S(1)} %get-tuple-element.25, f32[256,2,6]{0,2,1:T(8,128)S(1)} %get-tuple-element.18, pred[256,1024]{0,1:T(8,128)(4,1)S(1)} %broadcast_compare_fusion, f32[256,2,6]{0,2,1:T(8,128)S(1)} %get-tuple-element.9, ...), kind=kOutput, calls=%fused_computation.44 | convolution fusion | flops 819855360 | bytes 15794176 | tf_op jit(solution)/shard_map/tkgn,nkd->tkgd/dot_general | solution.py:137
  103.4 0.9 copy-done.6
  104.3 5.0 %fusion.78 = f32[256,1536]{1,0:T(8,128)} fusion(bf16[256,1536]{0,1:T(8,128)(2,1)S(1)} %bitcast.124, bf16[1536,1536]{1,0:T(8,128)(2,1)} %param.29), kind=kOutput, calls=%fused_computation.160 | convolution fusion | flops 1207959552 | bytes 7077888 | tf_op jit(solution)/shard_map/dot_general | solution.py:97
  109.3 4.3 %multiply_reduce_fusion.1 = (f32[256]{0:T(256)S(1)}, f32[256,1536]{1,0:T(8,128)}) fusion(f32[256,1536]{1,0:T(8,128)} %fusion.78, bf16[256,1536]{1,0:T(8,128)(2,1)} %param.33, bf16[256,1536]{0,1:T(8,128)(2,1)} %bitcast.125, bf16[1536,256]{1,0:T(8,128)(2,1)} %param.32, s32[256]{0:T(256)S(1)} %copy-done.23, s32[256]{0:T(256)S(1)} %copy-done.20, ...), kind=kOutput, calls=%fused_computation.49 | convolution fusion | flops 405602048 | bytes 6294528 | tf_op jit(solution)/shard_map/dot_general | solution.py:44
  113.6 1.6 multiply_convert_fusion
  115.3 6.2 %gather_fusion.2 = bf16[1536,1536]{1,0:T(8,128)(2,1)} fusion(bf16[256,1536]{1,0:T(8,128)(2,1)S(1)} %multiply_convert_fusion, s32[2048]{0:T(1024)S(1)} %pad_clamp_fusion), kind=kCustom, calls=%fused_computation.2 | custom fusion | bytes 9443328 | tf_op jit(solution)/shard_map/jit(_take)/gather | solution.py:240
  121.5 2.8 select_select_fusion
  124.2 61.3 %all_to_all.10 = bf16[32,48,1536]{2,1,0:T(8,128)(2,1)S(1)} all-to-all(bf16[32,48,1536]{2,1,0:T(8,128)(2,1)S(1)} %select_select_fusion), channel_id=1, replica_groups=mesh['req'=4,'exp'=32] {'exp'}, dimensions={0} | all-to-all | bytes 9437184 | tf_op jit(solution)/shard_map/all_to_all | solution.py:243
  185.6 9.7 %convolution_bitcast_fusion = f32[32,1,48,1536]{3,2,0,1:T(8,128)S(1)} fusion(bf16[32,48,1536]{2,1,0:T(8,128)(2,1)S(1)} %all_to_all.10, bf16[1,1536,1536]{2,1,0:T(8,128)(2,1)} %param.36), kind=kOutput, calls=%fused_computation.16 | convolution fusion | flops 7247757312 | bytes 18874368 | tf_op jit(solution)/shard_map/sxcd,xdf->sxcf/dot_general | solution.py:247
  195.3 5.5 %convolution_convert_fusion = bf16[32,48,1536]{2,1,0:T(8,128)(2,1)} fusion(f32[32,1,48,1536]{3,2,0,1:T(8,128)S(1)} %convolution_bitcast_fusion, bf16[1,768,1536]{2,1,0:T(8,128)(2,1)S(1)} %copy-done), kind=kOutput, calls=%fused_computation.22 | convolution fusion | flops 3629776896 | bytes 16515072 | tf_op jit(solution)/shard_map/sxcf,xfd->sxcd/dot_general | solution.py:252
  200.8 5.9 %all-to-all-start.1 = ((bf16[32,48,1536]{2,1,0:T(8,128)(2,1)}), bf16[32,48,1536]{2,1,0:T(8,128)(2,1)}, u32[]{:S(2)}, u32[]{:S(2)}) async-start(bf16[32,48,1536]{2,1,0:T(8,128)(2,1)} %convolution_convert_fusion), calls=%async_computation.1 | async-start | bytes 9437184 | tf_op jit(solution)/shard_map/all_to_all | solution.py:256
  208.0 8.7 %gather_fusion.4 = f32[1024]{0:T(1024)S(1)} fusion(f32[256,32]{0,1:T(8,128)S(1)} %fusion.79, s32[1024]{0:T(1024)S(1)} %reshape.466), kind=kCustom, calls=%fused_computation.4 | custom fusion | bytes 16384 | tf_op jit(solution)/shard_map/jit(take_along_axis)/gather | solution.py:108
  217.1 52.7 %all-to-all-done.1 = bf16[32,48,1536]{2,1,0:T(8,128)(2,1)} async-done(((bf16[32,48,1536]{2,1,0:T(8,128)(2,1)}), bf16[32,48,1536]{2,1,0:T(8,128)(2,1)}, u32[]{:S(2)}, u32[]{:S(2)}) %all-to-all-start.1) | async-done | bytes 4718624 | tf_op jit(solution)/shard_map/all_to_all | solution.py:256
  269.8 10.2 %gather_fusion.3 = bf16[1024,1536]{1,0:T(8,128)(2,1)} fusion(bf16[1536,1536]{1,0:T(8,128)(2,1)} %bitcast.31, s32[1024]{0:T(1024)S(1)} %broadcast_clamp_fusion), kind=kCustom, calls=%fused_computation.3 | custom fusion | bytes 6295552 | tf_op jit(solution)/shard_map/jit(_take)/gather | solution.py:257
  280.0 6.1 %gather.33 = bf16[256,4,1536]{2,1,0:T(4,128)(2,1)} reshape(bf16[1024,1536]{1,0:T(8,128)(2,1)} %gather_fusion.3) | data formatting | bytes 6291456 | tf_op jit(solution)/shard_map/jit(_take)/gather | solution.py:257
  286.2 16.2 %multiply_reduce_fusion = f32[256,1536]{1,0:T(8,128)S(1)} fusion(bf16[256,4,1536]{2,1,0:T(4,128)(2,1)} %gather.33, f32[256,4]{1,0:T(8,128)S(1)} %copy.110, pred[256,4]{1,0:T(8,128)(4,1)S(1)} %copy.116), kind=kLoop, calls=%fused_computation.10 | loop fusion | flops 5898240 | bytes 4723712 | tf_op jit(solution)/shard_map/reduce_sum | solution.py:259
  302.4 1.1 add_convert_fusion
  (108 shorter events, 12.5 us)
Async XLA Ops:
  6.5 188.8 %copy-start = (bf16[1,768,1536]{2,1,0:T(8,128)(2,1)S(1)}, bf16[1,768,1536]{2,1,0:T(8,128)(2,1)}, u32[]{:S(2)}) copy-start(bf16[1,768,1536]{2,1,0:T(8,128)(2,1)} %param.37) | copy-start | bytes 7077892
  6.5 25.1 %copy-start.4 = (bf16[256,1536]{1,0:T(8,128)(2,1)S(1)}, bf16[256,1536]{1,0:T(8,128)(2,1)}, u32[]{:S(2)}) copy-start(bf16[256,1536]{1,0:T(8,128)(2,1)} %param.19) | copy-start | bytes 2359300
  6.5 74.5 %all-gather.2.cloned.1.call-start = ((), (), s32[]{:S(2)}) async-start(), calls=%async_computation.2 | async-start | bytes 8454144 | tf_op jit(solution)/shard_map/all_gather | solution.py:201
  23.9 0.6 copy-start.14
  26.7 11.7 %copy-start.17 = (s32[1536]{0:T(1024)}, s32[1536]{0:T(1024)S(1)}, u32[]{:S(2)}) copy-start(s32[1536]{0:T(1024)S(1)} %select_reduce_fusion) | copy-start | bytes 18436
  28.4 14.9 %copy-start.19 = (s32[256]{0:T(256)}, s32[256]{0:T(256)S(1)}, u32[]{:S(2)}) copy-start(s32[256]{0:T(256)S(1)} %get-tuple-element.5) | copy-start | bytes 3076
  28.7 14.6 %copy-start.7 = (f32[256,64]{0,1:T(8,128)}, f32[256,64]{0,1:T(8,128)S(1)}, u32[]{:S(2)}) copy-start(f32[256,64]{0,1:T(8,128)S(1)} %get-tuple-element.20) | copy-start | bytes 196612
  28.8 14.6 %copy-start.9 = (f32[256,64]{0,1:T(8,128)}, f32[256,64]{0,1:T(8,128)S(1)}, u32[]{:S(2)}) copy-start(f32[256,64]{0,1:T(8,128)S(1)} %get-tuple-element.21) | copy-start | bytes 196612
  38.4 4.9 %copy-start.22 = (s32[256]{0:T(256)}, s32[256]{0:T(256)S(1)}, u32[]{:S(2)}) copy-start(s32[256]{0:T(256)S(1)} %and_select_fusion) | copy-start | bytes 3076
  47.4 3.2 %copy-start.8 = (f32[256,64]{0,1:T(8,128)S(1)}, f32[256,64]{0,1:T(8,128)}, u32[]{:S(2)}) copy-start(f32[256,64]{0,1:T(8,128)} %copy-done.7) | copy-start | bytes 196612
  47.4 3.2 %copy-start.10 = (f32[256,64]{0,1:T(8,128)S(1)}, f32[256,64]{0,1:T(8,128)}, u32[]{:S(2)}) copy-start(f32[256,64]{0,1:T(8,128)} %copy-done.9) | copy-start | bytes 196612
  65.1 23.1 %copy-start.21 = (pred[1024]{0:T(1024)(128)(4,1)S(1)}, pred[1024]{0:T(1024)(128)(4,1)}, u32[]{:S(2)}) copy-start(pred[1024]{0:T(1024)(128)(4,1)} %broadcast_in_dim.194) | copy-start | bytes 3076
  89.6 3.9 %copy-start.2 = (f32[2,256,256,6]{2,1,3,0:T(8,128)S(1)}, f32[2,256,256,6]{2,1,3,0:T(8,128)}, u32[]{:S(2)}) copy-start(f32[2,256,256,6]{2,1,3,0:T(8,128)} %get-tuple-element.23) | copy-start | bytes 9437188
  93.5 0.9 copy-start.11
  103.4 0.9 copy-start.6
  104.3 5.0 %copy-start.5 = (bf16[256,1536]{1,0:T(8,128)(2,1)S(1)}, bf16[256,1536]{1,0:T(8,128)(2,1)}, u32[]{:S(2)}) copy-start(bf16[256,1536]{1,0:T(8,128)(2,1)} %param.19) | copy-start | bytes 2359300
  104.3 5.0 %copy-start.20 = (s32[256]{0:T(256)S(1)}, s32[256]{0:T(256)}, u32[]{:S(2)}) copy-start(s32[256]{0:T(256)} %copy-done.19) | copy-start | bytes 3076
  104.3 5.0 %copy-start.23 = (s32[256]{0:T(256)S(1)}, s32[256]{0:T(256)}, u32[]{:S(2)}) copy-start(s32[256]{0:T(256)} %copy-done.22) | copy-start | bytes 3076
  109.3 4.4 %copy-start.16 = (f32[1536]{0:T(1024)S(1)}, f32[1536]{0:T(1024)}, u32[]{:S(2)}) copy-start(f32[1536]{0:T(1024)} %convert_element_type.97) | copy-start | bytes 18436
  115.3 6.2 %copy-start.18 = (pred[32,48]{1,0:T(8,128)(4,1)S(1)}, pred[32,48]{1,0:T(8,128)(4,1)}, u32[]{:S(2)}) copy-start(pred[32,48]{1,0:T(8,128)(4,1)} %broadcast_in_dim.200) | copy-start | bytes 4612
  200.8 5.9 %copy-start.15 = (s32[1024]{0:T(1024)S(1)}, s32[1024]{0:T(1024)}, u32[]{:S(2)}) copy-start(s32[1024]{0:T(1024)} %copy-done.14) | copy-start | bytes 12292
  200.8 6.0 %copy-start.12 = (s32[256,4]{0,1:T(4,128)S(1)}, s32[256,4]{0,1:T(4,128)}, u32[]{:S(2)}) copy-start(s32[256,4]{0,1:T(4,128)} %param.25) | copy-start | bytes 12292
  200.8 6.9 %copy-start.13 = (bf16[1536,32]{0,1:T(8,128)(2,1)S(1)}, bf16[1536,32]{0,1:T(8,128)(2,1)}, u32[]{:S(2)}) copy-start(bf16[1536,32]{0,1:T(8,128)(2,1)} %param.35) | copy-start | bytes 294916
  200.8 69.0 %all-to-all-start.1 = ((bf16[32,48,1536]{2,1,0:T(8,128)(2,1)}), bf16[32,48,1536]{2,1,0:T(8,128)(2,1)}, u32[]{:S(2)}, u32[]{:S(2)}) async-start(bf16[32,48,1536]{2,1,0:T(8,128)(2,1)} %convolution_convert_fusion), calls=%async_computation.1 | async-start | bytes 9437184 | tf_op jit(solution)/shard_map/all_to_all | solution.py:256
  286.2 16.3 %copy-start.3 = (f32[256,1536]{1,0:T(8,128)S(1)}, f32[256,1536]{1,0:T(8,128)}, u32[]{:S(2)}) copy-start(f32[256,1536]{1,0:T(8,128)} %get-tuple-element.27) | copy-start | bytes 4718596
  286.2 17.3 %copy-start.1 = (bf16[1,768,1536]{2,1,0:T(8,128)(2,1)S(1)}, bf16[1,768,1536]{2,1,0:T(8,128)(2,1)}, u32[]{:S(2)}) copy-start(bf16[1,768,1536]{2,1,0:T(8,128)(2,1)} %param.37) | copy-start | bytes 7077892
Sparse Core Ops, SparseCore 0:
  10.3 70.6 all-gather.1
where the time goes:
time: 312 us; the launch traced here: 310 us
  waiting for transfers between devices  69.4 us (22%)
  blocking collectives  61.3 us (20%)
  local copies, waits for them, and re-layouts  58.8 us (19%)
  matrix products  50.8 us (16%)
  other arithmetic  50.3 us (16%)
  between operations  13.9 us (4%)
  starting transfers between devices  5.86 us (2%)
    all_to_all x1, blocking collectives, on_device(): lax.all_to_all(outgoing, 'exp', split_axis=0, concat_axis=0, tiled=True)  61.3 us
    all_to_all x1, waiting for transfers between devices, on_device(): lax.all_to_all(result, 'exp', split_axis=0, concat_axis=0, tiled=True)  52.7 us
    gather x2, local copies, waits for them, and re-layouts, on_device(): jnp.take(returned.reshape(slot_total, -1), destination, axis=0)  16.3 us
    reduce_sum x1, other arithmetic, on_device(): jnp.sum(gates[..., None] * picked, axis=1)  16.2 us
    all_gather x1, waiting for transfers between devices, on_device(): lax.all_gather(shared_prompt_cache, ('req', 'exp'), axis=0, tiled=True)  15.9 us
    another operation x5, other arithmetic  12.5 us
    dot_general x1, matrix products, on_device(): jnp.einsum('sxcd,xdf->sxcf', arranged, expert_gate_up, preferred_element_...  9.72 us
    gather x5, local copies, waits for them, and re-layouts, gate_weights(): picked = jnp.take_along_axis(logits, routes, axis=1)  9.13 us
  transfers between devices with their start and end apart: 2, of which 2 were waited for; matrix products, arithmetic and copies ran while one was open for 22% of the time, Pallas kernels for 0%

commit v1 on v0

--- a/solution.py
+++ b/solution.py
@@ -13,6 +13,14 @@
 EPSILON = 1e-06
 THETA = 1000000.0
 VERY_NEGATIVE = -1e30
+
+
+def clear_side_over_axis(obj, row_axis):
+    main = jnp.concatenate(
+        lax.all_to_all(jnp.stack([obj for _ in range(lax.axis_size(row_axis))]), row_axis, 0, 0),
+        axis=0,
+    )
+    return main
 
 
 def rms_norm(weight_matrix, gain_vector):
@@ -198,7 +206,7 @@
     requested_pages = jnp.take(prompt_page_table.reshape(-1, PPP), request_prompt, axis=0).reshape(
         -1
     )
-    complete_cache = lax.all_gather(shared_prompt_cache, ("req", "exp"), axis=0, tiled=True)
+    complete_cache = clear_side_over_axis(shared_prompt_cache, ("req", "exp"))
     page_token_rows = jnp.take(complete_cache, requested_pages, axis=0).reshape(
         request_slot_count * PROMPT_LENGTH, 2 * KEY_VALUE_HEADS, HEAD_WIDTH
     )

time: 312 us -> 344 us (1.10)
  waiting for transfers between devices: 69.4 us -> 105 us
  between operations: 13.9 us -> 0.6 us
  starting transfers between devices: 5.86 us -> 16.5 us
  local copies, waits for them, and re-layouts: 58.8 us -> 62.8 us
  other arithmetic: 50.3 us -> 46.4 us
    all_to_all x0 -> x1, waiting for transfers between devices: none -> 51.8 us  [clear_side_over_axis(): lax.all_to_all(jnp.stack([obj for _ in range(lax.axis_size(row_axis))]),...]
    all_gather x1 -> x0, waiting for transfers between devices: 15.9 us -> none  [on_device(): lax.all_gather(shared_prompt_cache, ('req', 'exp'), axis=0, tiled=True)]
    all_to_all x0 -> x1, starting transfers between devices: none -> 10.7 us  [clear_side_over_axis(): lax.all_to_all(jnp.stack([obj for _ in range(lax.axis_size(row_axis))]),...]
    another operation x4 -> x5, local copies, waits for them, and re-layouts: 2.61 us -> 7.88 us  [the longest x1 5.27 us: clear_side_over_axis(): jnp.stack([obj for _ in range(lax.axis_size(row_axis))])]
  transfers between devices with their start and end apart: 2 -> 2, of which waited for: 2 -> 2; matrix products, arithmetic and copies ran while one was open for 22% -> 18% of each run, Pallas kernels for 0% -> 0%
where the time goes in v1:
time: 344 us; the launch traced here: 343 us
  waiting for transfers between devices  105 us (31%)
  local copies, waits for them, and re-layouts  62.8 us (18%)
  blocking collectives  61.6 us (18%)
  matrix products  50.7 us (15%)
  other arithmetic  46.4 us (13%)
  starting transfers between devices  16.5 us (5%)
    all_to_all x1, blocking collectives, on_device(): lax.all_to_all(outgoing, 'exp', split_axis=0, concat_axis=0, tiled=True)  61.6 us
    all_to_all x1, waiting for transfers between devices, on_device(): lax.all_to_all(result, 'exp', split_axis=0, concat_axis=0, tiled=True)  52.8 us
    all_to_all x1, waiting for transfers between devices, clear_side_over_axis(): lax.all_to_all(jnp.stack([obj for _ in range(lax.axis_size(row_axis))]),...  51.8 us
    gather x2, local copies, waits for them, and re-layouts, on_device(): jnp.take(returned.reshape(slot_total, -1), destination, axis=0)  16.3 us
    reduce_sum x1, other arithmetic, on_device(): jnp.sum(gates[..., None] * picked, axis=1)  16.2 us
    another operation x5, other arithmetic  12.5 us
    all_to_all x1, starting transfers between devices, clear_side_over_axis(): lax.all_to_all(jnp.stack([obj for _ in range(lax.axis_size(row_axis))]),...  10.7 us
    dot_general x1, matrix products, on_device(): jnp.einsum('sxcd,xdf->sxcf', arranged, expert_gate_up, preferred_element_...  9.72 us
  transfers between devices with their start and end apart: 2, of which 2 were waited for; matrix products, arithmetic and copies ran while one was open for 18% of the time, Pallas kernels for 0%

profile of v1, /device:TPU:32, one launch (start us, length us, event | category | flops | bytes accessed | tf_op | source)
XLA Modules:
  0.0 343.2 jit_solution(6650079622471130804)
XLA Ops:
  0.0 5.3 %stack.2 = bf16[128,4,16,512]{3,2,1,0:T(8,128)(2,1)} broadcast(bf16[4,16,512]{2,1,0:T(8,128)(2,1)} %param.24), dimensions={1,2,3} | broadcast | bytes 8454144 | tf_op jit(solution)/shard_map/stack | solution.py:20
  5.3 10.7 %all-to-all-start = ((bf16[128,4,16,512]{3,2,1,0:T(8,128)(2,1)}), bf16[128,4,16,512]{3,2,1,0:T(8,128)(2,1)}, u32[]{:S(2)}, u32[]{:S(2)}) async-start(bf16[128,4,16,512]{3,2,1,0:T(8,128)(2,1)} %stack.2), calls=%async_computation | async-start | bytes 16777216 | tf_op jit(solution)/shard_map/all_to_all | solution.py:20
  18.7 9.0 %reduce-window.6 = s32[32,8,128]{2,1,0:T(8,128)S(1)} reduce-window(s32[32,8,128]{2,1,0:T(8,128)S(1)} %fusion.53, s32[]{:T(128)} %constant.133.clone.1), window={size=1x1x128 pad=0_0x0_0x127_0}, to_apply=%region_10.11 | reduce-window | flops 4161536 | bytes 262148 | tf_op jit(solution)/shard_map/reduce-window
  28.2 0.8 fusion.3
  29.7 0.7 select_reduce_fusion
  31.7 0.7 copy.75
  32.4 0.7 copy.77
  33.4 2.8 fusion.75
  36.2 2.0 reshape.429
  38.2 1.2 slice.62
  39.4 0.7 copy.106
  40.2 4.9 %fusion.73 = f32[256,1536]{1,0:T(8,128)} fusion(bf16[1536,1536]{1,0:T(8,128)(2,1)} %param.27, bf16[256,1536]{1,0:T(8,128)(2,1)S(1)} %copy-done.4, f32[1536]{0:T(1024)S(1)} %convert_element_type.85, f32[256]{0:T(256)S(1)} %add_rsqrt_fusion.1), kind=kOutput, calls=%fused_computation.157 | convolution fusion | flops 1209532416 | bytes 7085056 | tf_op jit(solution)/shard_map/dot_general | solution.py:80
  45.1 4.1 %convolution_add_fusion.1 = f32[256,1536]{1,0:T(8,128)} fusion(f32[256,1536]{1,0:T(8,128)} %fusion.73, bf16[256,1536]{1,0:T(8,128)(2,1)} %param.31, bf16[1536,256]{1,0:T(8,128)(2,1)} %param.30, s32[256]{0:T(256)S(1)} %and_select_fusion, s32[256]{0:T(256)S(1)} %get-tuple-element.5, bf16[256,1536]{1,0:T(8,128)(2,1)S(1)} %copy-done.4, ...), kind=kOutput, calls=%fused_computation.27 | convolution fusion | flops 404815872 | bytes 5514240 | tf_op jit(solution)/shard_map/dot_general | solution.py:52
  49.2 3.1 copy.78
  52.3 2.3 subtract_convert_fusion
  54.6 1.4 copy.79
  56.0 1.2 copy.80
  57.1 0.7 fusion.54
  59.1 1.3 compare_and_fusion
  60.4 0.9 fusion.38
  61.3 0.9 broadcast_compare_fusion
  62.2 1.6 fusion.77
  63.8 1.0 subtract_convert_fusion.1
  64.8 3.8 %fusion.14 = (f32[256,2,6]{0,2,1:T(8,128)S(1)}, f32[2,256,256,6]{2,1,3,0:T(8,128)}) fusion(pred[256,256]{0,1:T(8,128)(4,1)S(1)} %fusion.38, bf16[256,2,6,64]{3,0,2,1:T(8,128)(2,1)} %bitcast.122, bf16[256,2,6,64]{3,0,2,1:T(8,128)(2,1)S(1)} %bitcast.120, bf16[256,2,64]{2,0,1:T(8,128)(2,1)S(1)} %get-tuple-element.14, bf16[256,2,64]{2,0,1:T(8,128)(2,1)S(1)} %get-tuple-element.13), kind=kOutput, calls=%fused_computation.32 | convolution fusion | flops 205517824 | bytes 4141056 | tf_op jit(solution)/shard_map/tkgd,nkd->tkgn/dot_general | solution.py:135
  68.6 51.8 %all-to-all-done = bf16[128,4,16,512]{3,2,1,0:T(8,128)(2,1)} async-done(((bf16[128,4,16,512]{3,2,1,0:T(8,128)(2,1)}), bf16[128,4,16,512]{3,2,1,0:T(8,128)(2,1)}, u32[]{:S(2)}, u32[]{:S(2)}) %all-to-all-start) | async-done | bytes 8388640 | tf_op jit(solution)/shard_map/all_to_all | solution.py:20
  120.4 5.1 %gather_fusion.1 = bf16[64,16,512]{2,1,0:T(8,128)(2,1)} fusion(bf16[512,16,512]{2,1,0:T(8,128)(2,1)} %bitcast.10, s32[1024]{0:T(1024)S(1)} %pad_clamp_fusion.1), kind=kCustom, calls=%fused_computation.1 | custom fusion | bytes 2097408 | tf_op jit(solution)/shard_map/jit(_take)/gather | solution.py:210
  125.5 2.1 gather.28
  127.6 1.4 copy_select_fusion
  129.1 3.8 %fusion.2 = (f32[256,2,6]{0,2,1:T(8,128)S(1)}, f32[2,1024,256,6]{2,1,3,0:T(8,128)S(1)}) fusion(pred[256,1024]{0,1:T(8,128)(4,1)S(1)} %broadcast_compare_fusion, bf16[256,2,6,64]{3,0,2,1:T(8,128)(2,1)} %bitcast.123, bf16[256,2,6,64]{3,0,2,1:T(8,128)(2,1)S(1)} %bitcast.121, bf16[1024,4,128]{2,0,1:T(8,128)(2,1)S(1)} %copy_select_fusion), kind=kOutput, calls=%fused_computation.9 | convolution fusion | flops 816313344 | bytes 14561280 | tf_op jit(solution)/shard_map/tkgd,nkd->tkgn/dot_general | solution.py:135
  133.8 2.1 fusion.22
  135.8 2.5 fusion
  138.4 4.4 %fusion.25 = bf16[256,2,6,128]{0,3,2,1:T(8,128)(2,1)S(1)} fusion(f32[2,128,256,6]{2,1,3,0:T(8,128)} %fusion.22, f32[2,1024,256,6]{2,1,3,0:T(8,128)S(1)} %get-tuple-element.25, f32[256,2,6]{0,2,1:T(8,128)S(1)} %get-tuple-element.18, pred[256,1024]{0,1:T(8,128)(4,1)S(1)} %broadcast_compare_fusion, f32[256,2,6]{0,2,1:T(8,128)S(1)} %get-tuple-element.9, ...), kind=kOutput, calls=%fused_computation.44 | convolution fusion | flops 819855360 | bytes 15794176 | tf_op jit(solution)/shard_map/tkgn,nkd->tkgd/dot_general | solution.py:145
  142.8 0.9 copy-done.6
  143.7 5.0 %fusion.78 = f32[256,1536]{1,0:T(8,128)} fusion(bf16[256,1536]{0,1:T(8,128)(2,1)S(1)} %bitcast.125, bf16[1536,1536]{1,0:T(8,128)(2,1)} %param.29), kind=kOutput, calls=%fused_computation.160 | convolution fusion | flops 1207959552 | bytes 7077888 | tf_op jit(solution)/shard_map/dot_general | solution.py:105
  148.7 4.3 %multiply_reduce_fusion.1 = (f32[256]{0:T(256)S(1)}, f32[256,1536]{1,0:T(8,128)}) fusion(f32[256,1536]{1,0:T(8,128)} %fusion.78, bf16[256,1536]{1,0:T(8,128)(2,1)} %param.33, bf16[256,1536]{0,1:T(8,128)(2,1)} %bitcast.126, bf16[1536,256]{1,0:T(8,128)(2,1)} %param.32, s32[256]{0:T(256)S(1)} %copy-done.25, s32[256]{0:T(256)S(1)} %copy-done.20, ...), kind=kOutput, calls=%fused_computation.49 | convolution fusion | flops 405602048 | bytes 6294528 | tf_op jit(solution)/shard_map/dot_general | solution.py:52
  153.0 1.6 multiply_convert_fusion
  154.7 6.2 %gather_fusion.2 = bf16[1536,1536]{1,0:T(8,128)(2,1)} fusion(bf16[256,1536]{1,0:T(8,128)(2,1)S(1)} %multiply_convert_fusion, s32[2048]{0:T(1024)S(1)} %copy-done.14), kind=kCustom, calls=%fused_computation.2 | custom fusion | bytes 9443328 | tf_op jit(solution)/shard_map/jit(_take)/gather | solution.py:248
  160.9 2.8 select_select_fusion
  163.7 61.6 %all_to_all.15 = bf16[32,48,1536]{2,1,0:T(8,128)(2,1)S(1)} all-to-all(bf16[32,48,1536]{2,1,0:T(8,128)(2,1)S(1)} %select_select_fusion), channel_id=1, replica_groups=mesh['req'=4,'exp'=32] {'exp'}, dimensions={0} | all-to-all | bytes 9437184 | tf_op jit(solution)/shard_map/all_to_all | solution.py:251
  225.3 9.7 %convolution_bitcast_fusion = f32[32,1,48,1536]{3,2,0,1:T(8,128)S(1)} fusion(bf16[32,48,1536]{2,1,0:T(8,128)(2,1)S(1)} %all_to_all.15, bf16[1,1536,1536]{2,1,0:T(8,128)(2,1)} %param.36), kind=kOutput, calls=%fused_computation.16 | convolution fusion | flops 7247757312 | bytes 18874368 | tf_op jit(solution)/shard_map/sxcd,xdf->sxcf/dot_general | solution.py:255
  235.0 5.5 %convolution_convert_fusion = bf16[32,48,1536]{2,1,0:T(8,128)(2,1)} fusion(f32[32,1,48,1536]{3,2,0,1:T(8,128)S(1)} %convolution_bitcast_fusion, bf16[1,768,1536]{2,1,0:T(8,128)(2,1)S(1)} %copy-done), kind=kOutput, calls=%fused_computation.22 | convolution fusion | flops 3629776896 | bytes 16515072 | tf_op jit(solution)/shard_map/sxcf,xfd->sxcd/dot_general | solution.py:260
  240.5 5.9 %all-to-all-start.2 = ((bf16[32,48,1536]{2,1,0:T(8,128)(2,1)}), bf16[32,48,1536]{2,1,0:T(8,128)(2,1)}, u32[]{:S(2)}, u32[]{:S(2)}) async-start(bf16[32,48,1536]{2,1,0:T(8,128)(2,1)} %convolution_convert_fusion), calls=%async_computation.2 | async-start | bytes 9437184 | tf_op jit(solution)/shard_map/all_to_all | solution.py:264
  247.7 8.7 %gather_fusion.4 = f32[1024]{0:T(1024)S(1)} fusion(f32[256,32]{0,1:T(8,128)S(1)} %fusion.79, s32[1024]{0:T(1024)S(1)} %reshape.472), kind=kCustom, calls=%fused_computation.4 | custom fusion | bytes 16384 | tf_op jit(solution)/shard_map/jit(take_along_axis)/gather | solution.py:116
  256.8 52.8 %all-to-all-done.2 = bf16[32,48,1536]{2,1,0:T(8,128)(2,1)} async-done(((bf16[32,48,1536]{2,1,0:T(8,128)(2,1)}), bf16[32,48,1536]{2,1,0:T(8,128)(2,1)}, u32[]{:S(2)}, u32[]{:S(2)}) %all-to-all-start.2) | async-done | bytes 4718624 | tf_op jit(solution)/shard_map/all_to_all | solution.py:264
  309.5 10.2 %gather_fusion.3 = bf16[1024,1536]{1,0:T(8,128)(2,1)} fusion(bf16[1536,1536]{1,0:T(8,128)(2,1)} %bitcast.32, s32[1024]{0:T(1024)S(1)} %broadcast_clamp_fusion), kind=kCustom, calls=%fused_computation.3 | custom fusion | bytes 6295552 | tf_op jit(solution)/shard_map/jit(_take)/gather | solution.py:265
  319.8 6.1 %gather.33 = bf16[256,4,1536]{2,1,0:T(4,128)(2,1)} reshape(bf16[1024,1536]{1,0:T(8,128)(2,1)} %gather_fusion.3) | data formatting | bytes 6291456 | tf_op jit(solution)/shard_map/jit(_take)/gather | solution.py:265
  325.9 16.2 %multiply_reduce_fusion = f32[256,1536]{1,0:T(8,128)S(1)} fusion(bf16[256,4,1536]{2,1,0:T(4,128)(2,1)} %gather.33, f32[256,4]{1,0:T(8,128)S(1)} %copy.88, pred[256,4]{1,0:T(8,128)(4,1)S(1)} %copy.94), kind=kLoop, calls=%fused_computation.10 | loop fusion | flops 5898240 | bytes 4723712 | tf_op jit(solution)/shard_map/reduce_sum | solution.py:267
  342.1 1.1 add_convert_fusion
  (118 shorter events, 9.0 us)
Async XLA Ops:
  0.0 235.0 %copy-start = (bf16[1,768,1536]{2,1,0:T(8,128)(2,1)S(1)}, bf16[1,768,1536]{2,1,0:T(8,128)(2,1)}, u32[]{:S(2)}) copy-start(bf16[1,768,1536]{2,1,0:T(8,128)(2,1)} %param.37) | copy-start | bytes 7077892
  5.3 10.8 %copy-start.26 = (s32[512]{0:T(512)S(1)}, s32[512]{0:T(512)}, u32[]{:S(2)}) copy-start(s32[512]{0:T(512)} %param.23) | copy-start | bytes 6148
  5.3 10.8 %copy-start.28 = (s32[4]{0:T(128)S(1)}, s32[4]{0:T(128)}, u32[]{:S(2)}) copy-start(s32[4]{0:T(128)} %param.21) | copy-start | bytes 52
  5.3 12.2 %copy-start.12 = (s32[256,4]{0,1:T(4,128)S(1)}, s32[256,4]{0,1:T(4,128)}, u32[]{:S(2)}) copy-start(s32[256,4]{0,1:T(4,128)} %param.25) | copy-start | bytes 12292
  5.3 12.6 %copy-start.22 = (bf16[1536]{0:T(1024)(128)(2,1)S(1)}, bf16[1536]{0:T(1024)(128)(2,1)}, u32[]{:S(2)}) copy-start(bf16[1536]{0:T(1024)(128)(2,1)} %param.26) | copy-start | bytes 9220
  5.3 12.6 %copy-start.23 = (bf16[1536]{0:T(1024)(128)(2,1)S(1)}, bf16[1536]{0:T(1024)(128)(2,1)}, u32[]{:S(2)}) copy-start(bf16[1536]{0:T(1024)(128)(2,1)} %param.34) | copy-start | bytes 9220
  5.3 25.8 %copy-start.18 = (s32[1,256]{1,0:T(1,128)S(1)}, s32[1,256]{1,0:T(1,128)}, u32[]{:S(2)}) copy-start(s32[1,256]{1,0:T(1,128)} %param.20) | copy-start | bytes 3076
  5.3 25.9 %copy-start.27 = (s32[4]{0:T(128)S(1)}, s32[4]{0:T(128)}, u32[]{:S(2)}) copy-start(s32[4]{0:T(128)} %param.22) | copy-start | bytes 52
  5.3 27.8 %copy-start.4 = (bf16[256,1536]{1,0:T(8,128)(2,1)S(1)}, bf16[256,1536]{1,0:T(8,128)(2,1)}, u32[]{:S(2)}) copy-start(bf16[256,1536]{1,0:T(8,128)(2,1)} %param.19) | copy-start | bytes 2359300
  5.3 115.1 %all-to-all-start = ((bf16[128,4,16,512]{3,2,1,0:T(8,128)(2,1)}), bf16[128,4,16,512]{3,2,1,0:T(8,128)(2,1)}, u32[]{:S(2)}, u32[]{:S(2)}) async-start(bf16[128,4,16,512]{3,2,1,0:T(8,128)(2,1)} %stack.2), calls=%async_computation | async-start | bytes 16777216 | tf_op jit(solution)/shard_map/all_to_all | solution.py:20
  30.4 9.7 %copy-start.15 = (s32[1536]{0:T(1024)}, s32[1536]{0:T(1024)S(1)}, u32[]{:S(2)}) copy-start(s32[1536]{0:T(1024)S(1)} %select_reduce_fusion) | copy-start | bytes 18436
  31.3 13.8 %copy-start.19 = (s32[256]{0:T(256)}, s32[256]{0:T(256)S(1)}, u32[]{:S(2)}) copy-start(s32[256]{0:T(256)S(1)} %get-tuple-element.5) | copy-start | bytes 3076
  31.7 13.4 %copy-start.7 = (f32[256,64]{0,1:T(8,128)}, f32[256,64]{0,1:T(8,128)S(1)}, u32[]{:S(2)}) copy-start(f32[256,64]{0,1:T(8,128)S(1)} %get-tuple-element.20) | copy-start | bytes 196612
  31.7 13.4 %copy-start.9 = (f32[256,64]{0,1:T(8,128)}, f32[256,64]{0,1:T(8,128)S(1)}, u32[]{:S(2)}) copy-start(f32[256,64]{0,1:T(8,128)S(1)} %get-tuple-element.21) | copy-start | bytes 196612
  40.2 4.9 %copy-start.24 = (s32[256]{0:T(256)}, s32[256]{0:T(256)S(1)}, u32[]{:S(2)}) copy-start(s32[256]{0:T(256)S(1)} %and_select_fusion) | copy-start | bytes 3076
  49.2 3.1 copy-start.8
  49.2 3.1 copy-start.10
  68.6 59.0 %copy-start.21 = (pred[1024]{0:T(1024)(128)(4,1)S(1)}, pred[1024]{0:T(1024)(128)(4,1)}, u32[]{:S(2)}) copy-start(pred[1024]{0:T(1024)(128)(4,1)} %broadcast_in_dim.194) | copy-start | bytes 3076
  129.1 3.9 %copy-start.2 = (f32[2,256,256,6]{2,1,3,0:T(8,128)S(1)}, f32[2,256,256,6]{2,1,3,0:T(8,128)}, u32[]{:S(2)}) copy-start(f32[2,256,256,6]{2,1,3,0:T(8,128)} %get-tuple-element.23) | copy-start | bytes 9437188
  132.9 0.9 copy-start.11
  142.8 0.9 copy-start.6
  143.7 5.0 %copy-start.5 = (bf16[256,1536]{1,0:T(8,128)(2,1)S(1)}, bf16[256,1536]{1,0:T(8,128)(2,1)}, u32[]{:S(2)}) copy-start(bf16[256,1536]{1,0:T(8,128)(2,1)} %param.19) | copy-start | bytes 2359300
  143.7 5.0 %copy-start.20 = (s32[256]{0:T(256)S(1)}, s32[256]{0:T(256)}, u32[]{:S(2)}) copy-start(s32[256]{0:T(256)} %copy-done.19) | copy-start | bytes 3076
  143.7 5.0 %copy-start.25 = (s32[256]{0:T(256)S(1)}, s32[256]{0:T(256)}, u32[]{:S(2)}) copy-start(s32[256]{0:T(256)} %copy-done.24) | copy-start | bytes 3076
  148.7 6.0 %copy-start.14 = (s32[2048]{0:T(1024)S(1)}, s32[2048]{0:T(1024)}, u32[]{:S(2)}) copy-start(s32[2048]{0:T(1024)} %pad_clamp_fusion) | copy-start | bytes 24580
  154.7 6.2 %copy-start.16 = (pred[32,48]{1,0:T(8,128)(4,1)S(1)}, pred[32,48]{1,0:T(8,128)(4,1)}, u32[]{:S(2)}) copy-start(pred[32,48]{1,0:T(8,128)(4,1)} %compare_and_fusion) | copy-start | bytes 4612
  154.7 6.2 %copy-start.17 = (pred[32,48]{1,0:T(8,128)(4,1)S(1)}, pred[32,48]{1,0:T(8,128)(4,1)}, u32[]{:S(2)}) copy-start(pred[32,48]{1,0:T(8,128)(4,1)} %broadcast_in_dim.200) | copy-start | bytes 4612
  240.5 6.9 %copy-start.13 = (bf16[1536,32]{0,1:T(8,128)(2,1)S(1)}, bf16[1536,32]{0,1:T(8,128)(2,1)}, u32[]{:S(2)}) copy-start(bf16[1536,32]{0,1:T(8,128)(2,1)} %param.35) | copy-start | bytes 294916
  240.5 69.1 %all-to-all-start.2 = ((bf16[32,48,1536]{2,1,0:T(8,128)(2,1)}), bf16[32,48,1536]{2,1,0:T(8,128)(2,1)}, u32[]{:S(2)}, u32[]{:S(2)}) async-start(bf16[32,48,1536]{2,1,0:T(8,128)(2,1)} %convolution_convert_fusion), calls=%async_computation.2 | async-start | bytes 9437184 | tf_op jit(solution)/shard_map/all_to_all | solution.py:264
  325.9 16.3 %copy-start.3 = (f32[256,1536]{1,0:T(8,128)S(1)}, f32[256,1536]{1,0:T(8,128)}, u32[]{:S(2)}) copy-start(f32[256,1536]{1,0:T(8,128)} %get-tuple-element.27) | copy-start | bytes 4718596
  325.9 17.3 %copy-start.1 = (bf16[1,768,1536]{2,1,0:T(8,128)(2,1)S(1)}, bf16[1,768,1536]{2,1,0:T(8,128)(2,1)}, u32[]{:S(2)}) copy-start(bf16[1,768,1536]{2,1,0:T(8,128)(2,1)} %param.37) | copy-start | bytes 7077892
